TPU v7x, 32 devices: a whole 2x2x4 slice. The times are simulated.
32 devices in a mesh: phi: 4 (over y, core), eta: 8 (over z, x).
Axes of the slice: x: 2, y: 2, z: 4, core: 2. Of those that a mesh axis runs over, the one named last changes fastest.
Arguments:
- edges: bfloat16 [65536, 128], P(('phi', 'eta')), may hold values from -6 to 6
- cotangent: bfloat16 [65536, 128], P(('phi', 'eta')), may hold values from -6 to 6
- send_rows: int32 [32, 32, 32], P(('phi', 'eta')), may hold values from 0 to 2047
- send_count: int32 [32, 32], P(('phi', 'eta')), may hold values from 1 to 32, as said below
- trip_local: int32 [262144], P(('phi', 'eta')), may hold values from 0 to 2047
- trip_remote: int32 [262144], P(('phi', 'eta')), may hold values from 0 to 1023, as said below
- w_first: bfloat16 [384, 256], replicated, may hold values from -0.3125 to 0.3125
- bias_first: float32 [256], replicated, may hold values from -4 to 4
- w_second: bfloat16 [256, 128], replicated, may hold values from -0.375 to 0.375
Outputs:
- new_edges: bfloat16 [65536, 128], P(('phi', 'eta'))
- edge_grad: bfloat16 [65536, 128], P(('phi', 'eta'))
- grad_first: float32 [384, 256], replicated
- grad_bias: float32 [256], replicated
- grad_second: float32 [256, 128], replicated
Inputs may be any that keep to these rules, and one draw needn't show every extreme that they name: `send_count`: some destination device has every slot live from every source. `trip_remote`: each triplet names a live slot of a source device toward its own owner.
All inputs are finite; a program needn't handle non-finite values.
Results may differ from a plain program's by a relative error of at most 0.0053.
Values may be sent and summed in bfloat16 or wider, within the bound.
A program may use at most 128 MiB of HBM per device.

v0:
```python
import jax
import jax.numpy as jnp
from jax import lax
from jax.sharding import PartitionSpec as P


def silu_slope(pre):
    sig = jax.nn.sigmoid(pre)
    return sig * (1.0 + pre * (1.0 - sig))


def local(
    edges, cotangent, send_rows, send_count, trip_local, trip_remote, w_first, bias_first, w_second
):
    width = edges.shape[1]
    local_edges = edges.shape[0]
    n_phi = lax.axis_size("phi")
    n_eta = lax.axis_size("eta")
    ndev = n_phi * n_eta
    slots_per = send_rows.shape[2]
    rows = send_rows[0]
    live = jnp.arange(slots_per, dtype=jnp.int32)[None, :] < send_count[0][:, None]
    zero = jnp.zeros((), jnp.bfloat16)
    stacked = jnp.stack([edges, cotangent], axis=1)
    outgoing = jnp.where(live[:, :, None, None], stacked[rows], zero)
    arrived = lax.all_to_all(outgoing, ("phi", "eta"), split_axis=0, concat_axis=0, tiled=True)
    arrived = arrived.reshape(ndev * slots_per, 2, width)
    inner = edges[trip_local]
    inner_cot = cotangent[trip_local]
    outer_pair = arrived[trip_remote]
    outer = outer_pair[:, 0, :]
    outer_cot = outer_pair[:, 1, :]
    inner_f = inner.astype(jnp.float32)
    outer_f = outer.astype(jnp.float32)
    prod = (inner_f * outer_f).astype(jnp.bfloat16)
    joined = jnp.concatenate([inner, outer, prod], axis=1)
    pre = jnp.dot(joined, w_first, preferred_element_type=jnp.float32) + bias_first
    hidden = jax.nn.silu(pre).astype(jnp.bfloat16)
    message = jnp.dot(hidden, w_second, preferred_element_type=jnp.float32)
    dmsg = (inner_cot.astype(jnp.float32) + outer_cot.astype(jnp.float32)).astype(jnp.bfloat16)
    dpre = jnp.dot(dmsg, w_second.T, preferred_element_type=jnp.float32) * silu_slope(pre)
    dpre_b = dpre.astype(jnp.bfloat16)
    dx = jnp.dot(dpre_b, w_first.T, preferred_element_type=jnp.float32)
    d_inner = dx[:, :width] + dx[:, 2 * width :] * outer_f
    d_outer = dx[:, width : 2 * width] + dx[:, 2 * width :] * inner_f
    slot_msg = jax.ops.segment_sum(message, trip_remote, ndev * slots_per)
    slot_grad = jax.ops.segment_sum(d_outer, trip_remote, ndev * slots_per)
    slot_sums = (
        jnp.stack([slot_msg, slot_grad], axis=1)
        .astype(jnp.bfloat16)
        .reshape(ndev, slots_per, 2, width)
    )
    returned = lax.all_to_all(slot_sums, ("phi", "eta"), split_axis=0, concat_axis=0, tiled=True)
    returned = jnp.where(live[:, :, None, None], returned, zero)
    grad_second = jnp.dot(hidden.T, dmsg, preferred_element_type=jnp.float32)
    grad_first = jnp.dot(joined.T, dpre_b, preferred_element_type=jnp.float32)
    grad_bias = jnp.sum(dpre, axis=0)
    grad_first, grad_bias, grad_second = lax.psum(
        (grad_first, grad_bias, grad_second), ("phi", "eta")
    )
    local_msg = jax.ops.segment_sum(message, trip_local, local_edges)
    local_grad = jax.ops.segment_sum(d_inner, trip_local, local_edges)
    flat_rows = rows.reshape(-1)
    local_msg = local_msg.at[flat_rows].add(
        returned[:, :, 0, :].astype(jnp.float32).reshape(-1, width)
    )
    local_grad = local_grad.at[flat_rows].add(
        returned[:, :, 1, :].astype(jnp.float32).reshape(-1, width)
    )
    new_edges = (edges.astype(jnp.float32) + local_msg).astype(jnp.bfloat16)
    edge_grad = (cotangent.astype(jnp.float32) + local_grad).astype(jnp.bfloat16)
    return (new_edges, edge_grad, grad_first, grad_bias, grad_second)


def solution(mesh):
    in_specs = (
        P(("phi", "eta"), None),
        P(("phi", "eta"), None),
        P(("phi", "eta"), None, None),
        P(("phi", "eta"), None),
        P(("phi", "eta")),
        P(("phi", "eta")),
        P(),
        P(),
        P(),
    )
    out_specs = (P(("phi", "eta"), None), P(("phi", "eta"), None), P(), P(), P())
    return jax.shard_map(local, mesh=mesh, in_specs=in_specs, out_specs=out_specs, check_vma=False)
```

profile of v0, /device:TPU:0, one launch (start us, length us, event | category | flops | bytes accessed | tf_op | source)
XLA Modules:
  0.0 520.3 jit_solution(7421459561959832188)
XLA Ops:
  7.2 0.0 copy-start
  7.2 0.8 iota_compare_fusion
  8.0 0.7 compare_select_fusion.2
  8.7 0.1 reshape.125
  8.8 1.8 copy.21
  10.6 0.0 copy-start.11
  10.6 1.9 copy.20
  12.5 2.4 pad_maximum_fusion.3
  14.9 3.7 gather_fusion.1
  18.6 1.0 copy_select_fusion
  19.6 7.3 %all-to-all-start = ((bf16[32,32,2,128]{3,1,2,0:T(8,128)(2,1)}), bf16[32,32,2,128]{3,1,2,0:T(8,128)(2,1)S(1)}, u32[]{:S(2)}, u32[]{:S(2)}) async-start(bf16[32,32,2,128]{3,1,2,0:T(8,128)(2,1)} %copy_select_fusion), calls=%async_computation | async-start | bytes 1048576 | tf_op jit(solution)/shard_map/all_to_all | solution.py:26
  26.9 0.1 reshape_squeeze.3
  27.0 0.1 convert_element_type.55
  27.1 1.1 convert_element_type.68
  28.2 29.2 %gather_fusion = bf16[8192,128]{1,0:T(8,128)(2,1)} fusion(bf16[2048,128]{1,0:T(8,128)(2,1)S(1)} %copy-done.2, s32[8192]{0:T(1024)S(1)} %fusion.22), kind=kCustom, calls=%fused_computation | custom fusion | bytes 4227072 | tf_op jit(solution)/shard_map/gather | solution.py:28
  57.4 29.2 %gather_fusion.3 = bf16[8192,128]{1,0:T(8,128)(2,1)} fusion(bf16[2048,128]{1,0:T(8,128)(2,1)S(1)} %copy-done.3, s32[8192]{0:T(1024)S(1)} %fusion.22), kind=kCustom, calls=%fused_computation.3 | custom fusion | bytes 4227072 | tf_op jit(solution)/shard_map/gather | solution.py:29
  86.7 0.5 copy.23
  87.2 53.3 %gather_fusion.2 = bf16[8192,2,128]{2,1,0:T(2,128)(2,1)} fusion(bf16[1024,2,128]{2,1,0:T(2,128)(2,1)S(1)} %bitcast.30, s32[8192]{0:T(1024)S(1)} %fusion.23), kind=kCustom, calls=%fused_computation.2 | custom fusion | bytes 8421376 | tf_op jit(solution)/shard_map/gather | solution.py:30
  140.5 9.5 %slice_convert_fusion = (f32[8192,1,128]{2,1,0:T(1,128)}, bf16[8192,1,128]{2,1,0:T(2,128)(2,1)S(1)}) fusion(bf16[8192,2,128]{2,1,0:T(2,128)(2,1)} %gather_fusion.2), kind=kLoop, calls=%fused_computation.25 | loop fusion | flops 1048576 | bytes 10485760 | tf_op jit(solution)/shard_map/convert_element_type | solution.py:40
  150.1 0.8 fusion.3
  150.9 5.2 %multiply_convert_fusion = (bf16[8192,256]{1,0:T(8,128)(2,1)S(1)}, f32[8192,256]{1,0:T(8,128)}) fusion(f32[256]{0:T(256)S(1)} %copy-done.13, bf16[384,256]{1,0:T(8,128)(2,1)S(1)} %copy-done, bf16[8192,128]{1,0:T(8,128)(2,1)S(1)} %get-tuple-element.7, bf16[8192,128]{1,0:T(8,128)(2,1)S(1)} %get-tuple-element.8, bf16[8192,128]{1,0:T(8,128)(2,1)S(1)} %copy-done.5), kind=kOutput, calls=%fused_computation.12 | convolution fusion | flops 1642070016 | bytes 19072000 | tf_op jit(solution)/shard_map/dot_general | solution.py:37
  156.1 2.0 copy-done.4
  158.1 3.2 fusion.29
  161.3 45.1 %scatter_custom_fusion.1 = f32[1024,128]{1,0:T(8,128)} fusion(s32[8192]{0:T(1024)S(1)} %copy-done.12, f32[8192,128]{1,0:T(8,128)} %fusion.29, f32[]{:T(128)} %constant.11.clone.1), kind=kCustom, calls=%fused_computation.43 | custom fusion | flops 1048576 | bytes 524800 | tf_op jit(solution)/shard_map/scatter-add | solution.py:46
  206.4 1.8 convert.11
  208.2 7.9 %fusion.28 = (f32[256]{0:T(256)S(1)}, bf16[8192,256]{1,0:T(8,128)(2,1)S(1)}) fusion(f32[8192,256]{1,0:T(8,128)} %get-tuple-element.14, bf16[256,128]{1,0:T(8,128)(2,1)S(1)} %copy-done.10, f32[8192,128]{1,0:T(8,128)} %bitcast.31, bf16[8192,128]{1,0:T(8,128)(2,1)} %gather_fusion.3), kind=kOutput, calls=%fused_computation.57 | convolution fusion | flops 560987904 | bytes 18940928 | tf_op jit(solution)/shard_map/dot_general | solution.py:41
  216.1 1.9 copy-done.7
  218.0 6.9 %fusion.13 = f32[8192,384]{1,0:T(8,128)} fusion(bf16[384,256]{1,0:T(8,128)(2,1)S(1)} %copy-done, bf16[8192,256]{1,0:T(8,128)(2,1)S(1)} %get-tuple-element.16), kind=kOutput, calls=%fused_computation.32 | convolution fusion | flops 1610612736 | bytes 16973824 | tf_op jit(solution)/shard_map/dot_general | solution.py:43
  225.0 45.7 %scatter_custom_fusion.2 = f32[1024,128]{1,0:T(8,128)} fusion(s32[8192]{0:T(1024)S(1)} %copy-done.12, bf16[8192,128]{1,0:T(8,128)(2,1)S(1)} %copy-done.5, f32[8192,384]{1,0:T(8,128)} %fusion.13, f32[]{:T(128)} %constant.11.clone.1), kind=kCustom, calls=%fused_computation.19 | custom fusion | flops 4194304 | bytes 11010560 | tf_op jit(solution)/shard_map/scatter-add | solution.py:47
  270.7 1.1 convert.12
  271.8 1.0 pad_maximum_fusion.4
  272.8 0.9 copy.25
  273.6 6.0 %all-to-all-start.1 = ((bf16[32,32,2,128]{3,1,2,0:T(8,128)(2,1)}), bf16[32,32,2,128]{3,1,2,0:T(8,128)(2,1)}, u32[]{:S(2)}, u32[]{:S(2)}) async-start(bf16[32,32,2,128]{3,1,2,0:T(8,128)(2,1)} %copy.25), calls=%async_computation.1 | async-start | bytes 1048576 | tf_op jit(solution)/shard_map/all_to_all | solution.py:53
  279.6 0.0 all-reduce.3.cloned.1.call-start
  279.6 6.0 %fusion.26 = f32[256,128]{1,0:T(8,128)} fusion(bf16[8192,256]{1,0:T(8,128)(2,1)} %copy-done.4, f32[8192,128]{1,0:T(8,128)} %bitcast.32, bf16[8192,128]{1,0:T(8,128)(2,1)} %gather_fusion.3), kind=kOutput, calls=%fused_computation.55 | convolution fusion | flops 540016640 | bytes 10616832 | tf_op jit(solution)/shard_map/dot_general | solution.py:55
  285.7 44.7 %scatter_fusion = f32[2048,128]{1,0:T(8,128)S(1)} fusion(f32[2048,128]{1,0:T(8,128)S(1)} %convert_element_type.55, s32[8192]{0:T(1024)S(1)} %copy-done.9, f32[8192,128]{1,0:T(8,128)} %fusion.29), kind=kCustom, calls=%fused_computation.4 | custom fusion | flops 1048576 | bytes 12615680 | tf_op jit(solution)/shard_map/scatter-add | solution.py:61
  330.4 42.8 %scatter_custom_fusion.4 = f32[2048,128]{1,0:T(8,128)} fusion(f32[2048,128]{1,0:T(8,128)} %convert_element_type.68, s32[8192]{0:T(1024)S(1)} %copy-done.9, bf16[8192,128]{1,0:T(8,128)(2,1)} %copy-done.6, f32[8192,384]{1,0:T(8,128)} %fusion.13), kind=kCustom, calls=%fused_computation.22 | custom fusion | flops 4194304 | bytes 11534336 | tf_op jit(solution)/shard_map/scatter-add | solution.py:62
  373.2 6.0 %fusion.11 = f32[384,256]{1,0:T(8,128)} fusion(bf16[8192,128]{1,0:T(8,128)(2,1)} %copy-done.8, bf16[8192,128]{1,0:T(8,128)(2,1)} %copy-done.6, bf16[8192,128]{1,0:T(8,128)(2,1)S(1)} %copy-done.5, bf16[8192,256]{1,0:T(8,128)(2,1)} %copy-done.7), kind=kOutput, calls=%fused_computation.29 | convolution fusion | flops 1629487104 | bytes 10878976 | tf_op jit(solution)/shard_map/dot_general | solution.py:56
  379.2 0.0 all-reduce.3.cloned.1.call-update
  379.2 40.6 %psum.22 = f32[256]{0:T(256)} all-reduce(f32[256]{0:T(256)S(1)} %get-tuple-element.15), channel_id=1, replica_groups=mesh['phi'=4,'eta'=8] {'phi','eta'}, use_global_device_ids=true, to_apply=%region_8.9 | all-reduce | flops 256 | bytes 2048 | tf_op jit(solution)/shard_map/psum | solution.py:58
  419.8 1.3 broadcast_select_fusion
  421.2 7.7 %scatter_custom_fusion.5 = f32[2048,128]{1,0:T(8,128)} fusion(f32[2048,128]{1,0:T(8,128)} %scatter_custom_fusion.4, s32[1024]{0:T(1024)S(1)} %bitcast.38, bf16[1024,128]{1,0:T(8,128)(2,1)S(1)} %bitcast.36), kind=kCustom, calls=%fused_computation.36 | custom fusion | flops 262144 | bytes 1310720 | tf_op jit(solution)/shard_map/scatter-add | solution.py:67
  428.8 2.1 convert_element_type.71
  430.9 6.5 %scatter_custom_fusion.3 = f32[2048,128]{1,0:T(8,128)S(1)} fusion(f32[2048,128]{1,0:T(8,128)S(1)} %scatter_fusion, s32[1024]{0:T(1024)S(1)} %bitcast.39, bf16[1024,128]{1,0:T(8,128)(2,1)S(1)} %bitcast.35), kind=kCustom, calls=%fused_computation.38 | custom fusion | flops 262144 | bytes 1310720 | tf_op jit(solution)/shard_map/scatter-add | solution.py:64
  437.4 0.8 convert_element_type.67
  438.2 71.9 %all-reduce.3.cloned.1.call-done = (f32[384,256]{1,0:T(8,128)}, f32[256,128]{1,0:T(8,128)}) async-done(((f32[384,256]{1,0:T(8,128)}, f32[256,128]{1,0:T(8,128)}), (f32[384,256]{1,0:T(8,128)}, f32[256,128]{1,0:T(8,128)})) %all-reduce.3.cloned.1.call-update) | async-done | bytes 524304 | tf_op jit(solution)/shard_map/psum | solution.py:58
  510.1 1.8 copy.36
  511.9 1.6 copy.37
  (31 shorter events, 0.1 us)
Async XLA Ops:
  7.2 143.7 %copy-start = (bf16[384,256]{1,0:T(8,128)(2,1)S(1)}, bf16[384,256]{1,0:T(8,128)(2,1)}, u32[]{:S(2)}) copy-start(bf16[384,256]{1,0:T(8,128)(2,1)} %param.15) | copy-start | bytes 589828
  10.6 16.4 %copy-start.11 = (s32[1,32,32]{2,1,0:T(8,128)S(1)}, s32[1,32,32]{2,1,0:T(8,128)}, u32[]{:S(2)}) copy-start(s32[1,32,32]{2,1,0:T(8,128)} %param.11) | copy-start | bytes 12292
  10.6 16.5 %copy-start.2 = (bf16[2048,128]{1,0:T(8,128)(2,1)S(1)}, bf16[2048,128]{1,0:T(8,128)(2,1)}, u32[]{:S(2)}) copy-start(bf16[2048,128]{1,0:T(8,128)(2,1)} %param.9) | copy-start | bytes 1572868
  12.4 14.7 %copy-start.3 = (bf16[2048,128]{1,0:T(8,128)(2,1)S(1)}, bf16[2048,128]{1,0:T(8,128)(2,1)}, u32[]{:S(2)}) copy-start(bf16[2048,128]{1,0:T(8,128)(2,1)} %param.10) | copy-start | bytes 1572868
  12.5 15.7 %copy-start.9 = (s32[8192]{0:T(1024)S(1)}, s32[8192]{0:T(1024)}, u32[]{:S(2)}) copy-start(s32[8192]{0:T(1024)} %param.13) | copy-start | bytes 98308
  19.6 67.1 %all-to-all-start = ((bf16[32,32,2,128]{3,1,2,0:T(8,128)(2,1)}), bf16[32,32,2,128]{3,1,2,0:T(8,128)(2,1)S(1)}, u32[]{:S(2)}, u32[]{:S(2)}) async-start(bf16[32,32,2,128]{3,1,2,0:T(8,128)(2,1)} %copy_select_fusion), calls=%async_computation | async-start | bytes 1048576 | tf_op jit(solution)/shard_map/all_to_all | solution.py:26
  57.4 29.2 %copy-start.12 = (s32[8192]{0:T(1024)S(1)}, s32[8192]{0:T(1024)}, u32[]{:S(2)}) copy-start(s32[8192]{0:T(1024)} %param.14) | copy-start | bytes 98308
  140.5 9.5 %copy-start.5 = (bf16[8192,128]{1,0:T(8,128)(2,1)S(1)}, bf16[8192,128]{1,0:T(8,128)(2,1)}, u32[]{:S(2)}) copy-start(bf16[8192,128]{1,0:T(8,128)(2,1)} %gather_fusion) | copy-start | bytes 6291460
  150.1 0.9 copy-start.13
  150.9 5.3 %copy-start.6 = (bf16[8192,128]{1,0:T(8,128)(2,1)}, bf16[8192,128]{1,0:T(8,128)(2,1)S(1)}, u32[]{:S(2)}) copy-start(bf16[8192,128]{1,0:T(8,128)(2,1)S(1)} %get-tuple-element.8) | copy-start | bytes 6291460
  150.9 5.3 %copy-start.8 = (bf16[8192,128]{1,0:T(8,128)(2,1)}, bf16[8192,128]{1,0:T(8,128)(2,1)S(1)}, u32[]{:S(2)}) copy-start(bf16[8192,128]{1,0:T(8,128)(2,1)S(1)} %get-tuple-element.7) | copy-start | bytes 6291460
  150.9 7.2 %copy-start.10 = (bf16[256,128]{1,0:T(8,128)(2,1)S(1)}, bf16[256,128]{1,0:T(8,128)(2,1)}, u32[]{:S(2)}) copy-start(bf16[256,128]{1,0:T(8,128)(2,1)} %param.17) | copy-start | bytes 196612
  156.1 2.0 copy-start.4
  216.1 1.9 copy-start.7
  273.6 146.2 %all-to-all-start.1 = ((bf16[32,32,2,128]{3,1,2,0:T(8,128)(2,1)}), bf16[32,32,2,128]{3,1,2,0:T(8,128)(2,1)}, u32[]{:S(2)}, u32[]{:S(2)}) async-start(bf16[32,32,2,128]{3,1,2,0:T(8,128)(2,1)} %copy.25), calls=%async_computation.1 | async-start | bytes 1048576 | tf_op jit(solution)/shard_map/all_to_all | solution.py:53
  279.6 230.5 %all-reduce.3.cloned.1.call-start = ((), (), s32[]{:S(2)}) async-start(), calls=%async_computation.2 | async-start | bytes 1048576 | tf_op jit(solution)/shard_map/psum | solution.py:58
  419.8 93.6 %copy-start.1 = (bf16[384,256]{1,0:T(8,128)(2,1)S(1)}, bf16[384,256]{1,0:T(8,128)(2,1)}, u32[]{:S(2)}) copy-start(bf16[384,256]{1,0:T(8,128)(2,1)} %param.15) | copy-start | bytes 589828
Sparse Core Ops, SparseCore 0:
  379.4 130.6 all-reduce.2
where the time goes:
time: 521 us; the launch traced here: 520 us
  other arithmetic  217 us (42%)
  local copies, waits for them, and re-layouts  128 us (25%)
  waiting for transfers between devices  71.9 us (14%)
  blocking collectives  40.6 us (8%)
  matrix products  35.3 us (7%)
  between operations  14.3 us (3%)
  starting transfers between devices  13.3 us (3%)
    psum x1, waiting for transfers between devices, local(): lax.psum((grad_first, grad_bias, grad_second), ('phi', 'eta'))  71.9 us
    gather x1, local copies, waits for them, and re-layouts, local(): outer_pair = arrived[trip_remote]  53.3 us
    scatter-add x1, other arithmetic, local(): slot_grad = jax.ops.segment_sum(d_outer, trip_remote, ndev * slots_per)  45.7 us
    scatter-add x1, other arithmetic, local(): slot_msg = jax.ops.segment_sum(message, trip_remote, ndev * slots_per)  45.1 us
    scatter-add x1, other arithmetic, local(): local_msg = jax.ops.segment_sum(message, trip_local, local_edges)  44.7 us
    scatter-add x1, other arithmetic, local(): local_grad = jax.ops.segment_sum(d_inner, trip_local, local_edges)  42.8 us
    psum x1, blocking collectives, local(): lax.psum((grad_first, grad_bias, grad_second), ('phi', 'eta'))  40.6 us
    gather x1, local copies, waits for them, and re-layouts, local(): inner_cot = cotangent[trip_local]  29.2 us
  transfers between devices with their start and end apart: 3, of which 1 were waited for; matrix products, arithmetic and copies ran while one was open for 34% of the time, Pallas kernels for 0%

commit v1 on v0

--- a/solution.py
+++ b/solution.py
@@ -56,7 +56,7 @@
     grad_first = jnp.dot(joined.T, dpre_b, preferred_element_type=jnp.float32)
     grad_bias = jnp.sum(dpre, axis=0)
     grad_first, grad_bias, grad_second = lax.psum(
-        (grad_first, grad_bias, grad_second), ("phi", "eta")
+        lax.psum((grad_first, grad_bias, grad_second), "eta"), "phi"
     )
     local_msg = jax.ops.segment_sum(message, trip_local, local_edges)
     local_grad = jax.ops.segment_sum(d_inner, trip_local, local_edges)

time: 521 us -> 441 us (0.85)
  waiting for transfers between devices: 71.9 us -> 15.2 us
  blocking collectives: 40.6 us -> 27.8 us
  matrix products: 35.3 us -> 28.4 us
    psum x1 -> x2, waiting for transfers between devices: 71.9 us -> 15.2 us  [the longest x1 15.2 us: local(): lax.psum(lax.psum((grad_first, grad_bias, grad_second), 'eta'), 'phi')]
    psum x1 -> x2, blocking collectives: 40.6 us -> 27.8 us  [the longest x1 21.6 us: local(): lax.psum((grad_first, grad_bias, grad_second), 'eta')]
  transfers between devices with their start and end apart: 3 -> 4, of which waited for: 1 -> 1; matrix products, arithmetic and copies ran while one was open for 34% -> 39% of each run, Pallas kernels for 0% -> 0%
where the time goes in v1:
time: 441 us
  other arithmetic  216 us (49%)
  local copies, waits for them, and re-layouts  125 us (28%)
  matrix products  28.4 us (6%)
  blocking collectives  27.8 us (6%)
  waiting for transfers between devices  15.2 us (3%)
  between operations  14.4 us (3%)
  starting transfers between devices  13.4 us (3%)
    gather x1, local copies, waits for them, and re-layouts, local(): outer_pair = arrived[trip_remote]  53.2 us
    scatter-add x1, other arithmetic, local(): slot_grad = jax.ops.segment_sum(d_outer, trip_remote, ndev * slots_per)  45.7 us
    scatter-add x1, other arithmetic, local(): local_grad = jax.ops.segment_sum(d_inner, trip_local, local_edges)  45.5 us
    scatter-add x1, other arithmetic, local(): slot_msg = jax.ops.segment_sum(message, trip_remote, ndev * slots_per)  45.2 us
    scatter-add x1, other arithmetic, local(): local_msg = jax.ops.segment_sum(message, trip_local, local_edges)  44.7 us
    gather x1, local copies, waits for them, and re-layouts, local(): inner = edges[trip_local]  29.2 us
    gather x1, local copies, waits for them, and re-layouts, local(): inner_cot = cotangent[trip_local]  29.2 us
    psum x1, blocking collectives, local(): lax.psum((grad_first, grad_bias, grad_second), 'eta')  21.6 us
  transfers between devices with their start and end apart: 4, of which 1 were waited for; matrix products, arithmetic and copies ran while one was open for 39% of the time, Pallas kernels for 0%

profile of v1, /device:TPU:0, one launch (start us, length us, event | category | flops | bytes accessed | tf_op | source)
XLA Modules:
  0.0 440.6 jit_solution(13191205977555992116)
XLA Ops:
  7.2 0.0 copy-start
  7.2 0.8 iota_compare_fusion
  7.9 1.8 copy.20
  9.8 1.9 copy.21
  11.6 0.7 compare_select_fusion.2
  12.4 0.1 reshape.125
  12.4 3.2 pad_maximum_fusion.3
  15.6 4.9 %gather_fusion.1 = bf16[1024,2,128]{2,1,0:T(2,128)(2,1)S(1)} fusion(bf16[2048,2,128]{2,1,0:T(2,128)(2,1)} %pad_maximum_fusion.3, s32[1024]{0:T(1024)S(1)} %broadcast_clamp_fusion), kind=kCustom, calls=%fused_computation.1 | custom fusion | bytes 1052672 | tf_op jit(solution)/shard_map/gather | solution.py:25
  20.6 1.0 copy_select_fusion
  21.6 7.5 %all-to-all-start = ((bf16[32,32,2,128]{3,1,2,0:T(8,128)(2,1)}), bf16[32,32,2,128]{3,1,2,0:T(8,128)(2,1)S(1)}, u32[]{:S(2)}, u32[]{:S(2)}) async-start(bf16[32,32,2,128]{3,1,2,0:T(8,128)(2,1)} %copy_select_fusion), calls=%async_computation | async-start | bytes 1048576 | tf_op jit(solution)/shard_map/all_to_all | solution.py:26
  29.1 29.2 %gather_fusion = bf16[8192,128]{1,0:T(8,128)(2,1)} fusion(bf16[2048,128]{1,0:T(8,128)(2,1)S(1)} %copy-done.2, s32[8192]{0:T(1024)S(1)} %fusion.22), kind=kCustom, calls=%fused_computation | custom fusion | bytes 4227072 | tf_op jit(solution)/shard_map/gather | solution.py:28
  58.3 29.2 %gather_fusion.3 = bf16[8192,128]{1,0:T(8,128)(2,1)} fusion(bf16[2048,128]{1,0:T(8,128)(2,1)S(1)} %copy-done.1, s32[8192]{0:T(1024)S(1)} %fusion.22), kind=kCustom, calls=%fused_computation.3 | custom fusion | bytes 4227072 | tf_op jit(solution)/shard_map/gather | solution.py:29
  87.6 0.5 copy.23
  88.1 53.2 %gather_fusion.2 = bf16[8192,2,128]{2,1,0:T(2,128)(2,1)} fusion(bf16[1024,2,128]{2,1,0:T(2,128)(2,1)S(1)} %bitcast.30, s32[8192]{0:T(1024)S(1)} %fusion.23), kind=kCustom, calls=%fused_computation.2 | custom fusion | bytes 8421376 | tf_op jit(solution)/shard_map/gather | solution.py:30
  141.3 8.7 %slice_convert_fusion = (f32[8192,1,128]{2,1,0:T(1,128)S(1)}, bf16[8192,1,128]{2,1,0:T(2,128)(2,1)S(1)}) fusion(bf16[8192,2,128]{2,1,0:T(2,128)(2,1)} %gather_fusion.2), kind=kLoop, calls=%fused_computation.25 | loop fusion | flops 1048576 | bytes 10485760 | tf_op jit(solution)/shard_map/convert_element_type | solution.py:40
  150.0 0.8 fusion.3
  150.9 4.2 multiply_convert_fusion
  155.1 3.9 fusion.28
  159.0 2.6 fusion.11
  161.6 6.9 %fusion.13 = f32[8192,384]{1,0:T(8,128)} fusion(bf16[384,256]{1,0:T(8,128)(2,1)S(1)} %copy-done, bf16[8192,256]{1,0:T(8,128)(2,1)S(1)} %get-tuple-element.18), kind=kOutput, calls=%fused_computation.32 | convolution fusion | flops 1610612736 | bytes 16973824 | tf_op jit(solution)/shard_map/dot_general | solution.py:43
  168.5 45.7 %scatter_custom_fusion.2 = f32[1024,128]{1,0:T(8,128)} fusion(s32[8192]{0:T(1024)S(1)} %copy-done.11, bf16[8192,128]{1,0:T(8,128)(2,1)S(1)} %copy-done.3, f32[8192,384]{1,0:T(8,128)} %fusion.13, f32[]{:T(128)} %constant.11.clone.1), kind=kCustom, calls=%fused_computation.19 | custom fusion | flops 4194304 | bytes 11010560 | tf_op jit(solution)/shard_map/scatter-add | solution.py:47
  214.3 1.8 convert.12
  216.0 5.4 %fusion.29 = f32[8192,128]{1,0:T(8,128)} fusion(bf16[8192,256]{1,0:T(8,128)(2,1)} %get-tuple-element.15, bf16[256,128]{1,0:T(8,128)(2,1)S(1)} %copy-done.9), kind=kOutput, calls=%fused_computation.58 | convolution fusion | flops 536870912 | bytes 8454144 | tf_op jit(solution)/shard_map/dot_general | solution.py:39
  221.4 45.2 %scatter_custom_fusion.1 = f32[1024,128]{1,0:T(8,128)} fusion(s32[8192]{0:T(1024)S(1)} %copy-done.11, f32[8192,128]{1,0:T(8,128)} %fusion.29, f32[]{:T(128)} %constant.11.clone.1), kind=kCustom, calls=%fused_computation.43 | custom fusion | flops 1048576 | bytes 524800 | tf_op jit(solution)/shard_map/scatter-add | solution.py:46
  266.7 1.1 convert.11
  267.7 1.0 pad_maximum_fusion.4
  268.7 0.9 copy.25
  269.6 5.8 %all-to-all-start.1 = ((bf16[32,32,2,128]{3,1,2,0:T(8,128)(2,1)}), bf16[32,32,2,128]{3,1,2,0:T(8,128)(2,1)}, u32[]{:S(2)}, u32[]{:S(2)}) async-start(bf16[32,32,2,128]{3,1,2,0:T(8,128)(2,1)} %copy.25), calls=%async_computation.1 | async-start | bytes 1048576 | tf_op jit(solution)/shard_map/all_to_all | solution.py:53
  275.4 0.0 all-reduce.5.cloned.1.call-start
  275.5 5.4 %fusion.26 = f32[256,128]{1,0:T(8,128)} fusion(bf16[8192,256]{1,0:T(8,128)(2,1)} %get-tuple-element.15, f32[8192,128]{1,0:T(8,128)} %bitcast.32, bf16[8192,128]{1,0:T(8,128)(2,1)S(1)} %copy-done.7), kind=kOutput, calls=%fused_computation.55 | convolution fusion | flops 540016640 | bytes 10616832 | tf_op jit(solution)/shard_map/dot_general | solution.py:55
  280.9 0.0 all-reduce.5.cloned.1.call-update
  280.9 0.0 all-reduce.7.cloned.1.call-start
  281.0 0.1 convert_element_type.68
  281.0 0.1 reshape_squeeze.3
  281.1 0.1 convert_element_type.55
  281.2 45.5 %scatter_custom_fusion.4 = f32[2048,128]{1,0:T(8,128)S(1)} fusion(f32[2048,128]{1,0:T(8,128)S(1)} %convert_element_type.68, s32[8192]{0:T(1024)S(1)} %copy-done.8, bf16[8192,128]{1,0:T(8,128)(2,1)} %copy-done.5, f32[8192,384]{1,0:T(8,128)} %fusion.13), kind=kCustom, calls=%fused_computation.22 | custom fusion | flops 4194304 | bytes 11534336 | tf_op jit(solution)/shard_map/scatter-add | solution.py:62
  326.7 44.7 %scatter_fusion = f32[2048,128]{1,0:T(8,128)S(1)} fusion(f32[2048,128]{1,0:T(8,128)S(1)} %convert_element_type.55, s32[8192]{0:T(1024)S(1)} %copy-done.8, f32[8192,128]{1,0:T(8,128)} %fusion.29), kind=kCustom, calls=%fused_computation.4 | custom fusion | flops 1048576 | bytes 12615680 | tf_op jit(solution)/shard_map/scatter-add | solution.py:61
  371.4 21.6 %psum.44 = f32[256]{0:T(256)S(1)} all-reduce(f32[256]{0:T(256)S(1)} %get-tuple-element.17), channel_id=1, replica_groups=mesh['phi'=4,'eta'=8] {'eta'}, use_global_device_ids=true, to_apply=%region_9.10 | all-reduce | flops 256 | bytes 2048 | tf_op jit(solution)/shard_map/psum | solution.py:59
  393.0 6.2 %psum.45 = f32[256]{0:T(256)} all-reduce(f32[256]{0:T(256)S(1)} %psum.44), channel_id=1, replica_groups=mesh['phi'=4,'eta'=8] {'phi'}, use_global_device_ids=true, to_apply=%region_10.11 | all-reduce | flops 256 | bytes 2048 | tf_op jit(solution)/shard_map/psum | solution.py:58
  399.2 0.0 all-reduce.7.cloned.1.call-update
  399.3 1.2 broadcast_select_fusion
  400.6 6.5 %scatter_custom_fusion.5 = f32[2048,128]{1,0:T(8,128)S(1)} fusion(f32[2048,128]{1,0:T(8,128)S(1)} %scatter_custom_fusion.4, s32[1024]{0:T(1024)S(1)} %bitcast.38, bf16[1024,128]{1,0:T(8,128)(2,1)S(1)} %bitcast.36), kind=kCustom, calls=%fused_computation.36 | custom fusion | flops 262144 | bytes 1310720 | tf_op jit(solution)/shard_map/scatter-add | solution.py:67
  407.0 0.8 convert_element_type.71
  407.9 6.5 %scatter_custom_fusion.3 = f32[2048,128]{1,0:T(8,128)S(1)} fusion(f32[2048,128]{1,0:T(8,128)S(1)} %scatter_fusion, s32[1024]{0:T(1024)S(1)} %bitcast.39, bf16[1024,128]{1,0:T(8,128)(2,1)S(1)} %bitcast.34), kind=kCustom, calls=%fused_computation.38 | custom fusion | flops 262144 | bytes 1310720 | tf_op jit(solution)/shard_map/scatter-add | solution.py:64
  414.3 0.8 convert_element_type.67
  415.2 15.2 %all-reduce.7.cloned.1.call-done = (f32[384,256]{1,0:T(8,128)}, f32[256,128]{1,0:T(8,128)}) async-done(((f32[384,256]{1,0:T(8,128)}, f32[256,128]{1,0:T(8,128)}), (f32[384,256]{1,0:T(8,128)}, f32[256,128]{1,0:T(8,128)})) %all-reduce.7.cloned.1.call-update) | async-done | bytes 524304 | tf_op jit(solution)/shard_map/psum | solution.py:58
  430.4 1.8 copy.38
  432.2 1.6 copy.39
  (33 shorter events, 0.1 us)
Async XLA Ops:
  7.2 143.7 %copy-start = (bf16[384,256]{1,0:T(8,128)(2,1)S(1)}, bf16[384,256]{1,0:T(8,128)(2,1)}, u32[]{:S(2)}) copy-start(bf16[384,256]{1,0:T(8,128)(2,1)} %param.15) | copy-start | bytes 589828
  9.7 19.3 %copy-start.8 = (s32[8192]{0:T(1024)S(1)}, s32[8192]{0:T(1024)}, u32[]{:S(2)}) copy-start(s32[8192]{0:T(1024)} %param.13) | copy-start | bytes 98308
  9.8 19.3 %copy-start.2 = (bf16[2048,128]{1,0:T(8,128)(2,1)S(1)}, bf16[2048,128]{1,0:T(8,128)(2,1)}, u32[]{:S(2)}) copy-start(bf16[2048,128]{1,0:T(8,128)(2,1)} %param.9) | copy-start | bytes 1572868
  21.6 66.0 %all-to-all-start = ((bf16[32,32,2,128]{3,1,2,0:T(8,128)(2,1)}), bf16[32,32,2,128]{3,1,2,0:T(8,128)(2,1)S(1)}, u32[]{:S(2)}, u32[]{:S(2)}) async-start(bf16[32,32,2,128]{3,1,2,0:T(8,128)(2,1)} %copy_select_fusion), calls=%async_computation | async-start | bytes 1048576 | tf_op jit(solution)/shard_map/all_to_all | solution.py:26
  29.1 29.2 %copy-start.1 = (bf16[2048,128]{1,0:T(8,128)(2,1)S(1)}, bf16[2048,128]{1,0:T(8,128)(2,1)}, u32[]{:S(2)}) copy-start(bf16[2048,128]{1,0:T(8,128)(2,1)} %param.10) | copy-start | bytes 1572868
  58.3 29.2 %copy-start.11 = (s32[8192]{0:T(1024)S(1)}, s32[8192]{0:T(1024)}, u32[]{:S(2)}) copy-start(s32[8192]{0:T(1024)} %param.14) | copy-start | bytes 98308
  141.3 8.7 %copy-start.3 = (bf16[8192,128]{1,0:T(8,128)(2,1)S(1)}, bf16[8192,128]{1,0:T(8,128)(2,1)}, u32[]{:S(2)}) copy-start(bf16[8192,128]{1,0:T(8,128)(2,1)} %gather_fusion) | copy-start | bytes 6291460
  150.0 5.1 %copy-start.4 = (f32[8192,1,128]{2,1,0:T(1,128)}, f32[8192,1,128]{2,1,0:T(1,128)S(1)}, u32[]{:S(2)}) copy-start(f32[8192,1,128]{2,1,0:T(1,128)S(1)} %get-tuple-element.11) | copy-start | bytes 12582916
  150.0 0.9 copy-start.12
  150.9 8.1 %copy-start.5 = (bf16[8192,128]{1,0:T(8,128)(2,1)}, bf16[8192,128]{1,0:T(8,128)(2,1)S(1)}, u32[]{:S(2)}) copy-start(bf16[8192,128]{1,0:T(8,128)(2,1)S(1)} %get-tuple-element.10) | copy-start | bytes 6291460
  150.9 4.2 copy-start.6
  150.9 4.2 copy-start.9
  221.4 54.0 %copy-start.7 = (bf16[8192,128]{1,0:T(8,128)(2,1)S(1)}, bf16[8192,128]{1,0:T(8,128)(2,1)}, u32[]{:S(2)}) copy-start(bf16[8192,128]{1,0:T(8,128)(2,1)} %gather_fusion.3) | copy-start | bytes 6291460
  269.6 129.7 %all-to-all-start.1 = ((bf16[32,32,2,128]{3,1,2,0:T(8,128)(2,1)}), bf16[32,32,2,128]{3,1,2,0:T(8,128)(2,1)}, u32[]{:S(2)}, u32[]{:S(2)}) async-start(bf16[32,32,2,128]{3,1,2,0:T(8,128)(2,1)} %copy.25), calls=%async_computation.1 | async-start | bytes 1048576 | tf_op jit(solution)/shard_map/all_to_all | solution.py:53
  275.4 5.6 %copy-start.10 = (s32[1,32,32]{2,1,0:T(8,128)S(1)}, s32[1,32,32]{2,1,0:T(8,128)}, u32[]{:S(2)}) copy-start(s32[1,32,32]{2,1,0:T(8,128)} %param.11) | copy-start | bytes 12292
  275.4 123.8 %all-reduce.5.cloned.1.call-start = ((), (), s32[]{:S(2)}) async-start(), calls=%async_computation.2 | async-start | bytes 1048576 | tf_op jit(solution)/shard_map/psum | solution.py:59
  280.9 149.5 %all-reduce.7.cloned.1.call-start = ((), (), s32[]{:S(2)}) async-start(), calls=%async_computation.3 | async-start | bytes 1048576 | tf_op jit(solution)/shard_map/psum | solution.py:58
Sparse Core Ops, SparseCore 0:
  281.0 73.8 all-reduce.4
  399.4 30.9 all-reduce.6
